TPU v7x, 32 devices: a whole 2x2x4 slice. The times are simulated.
32 devices in a mesh: aux: 4 (over y, x), blk: 4 (over z), occ: 2 (over core).
Axes of the slice: x: 2, y: 2, z: 4, core: 2. Of those that a mesh axis runs over, the one named last changes fastest.
Arguments:
- integrals: bfloat16 [16, 4, 11, 512, 512], P('aux', 'blk'), may hold values from -0.078125 to 0.078125
- orbitals: bfloat16 [2048, 512], P('blk', 'occ'), may hold values from -6 to 6
- pair_lists: int32 [4, 11], P('blk'), may hold values from 0 to 3, as said below
- pair_counts: int32 [4], P('blk'), may hold values from 1 to 11, as said below
Outputs:
- exchange: float32 [4, 512, 512], P('blk', 'aux')
Inputs may be any that keep to these rules, and one draw needn't show every extreme that they name: `pair_lists`: entry 0 of row m is m itself; entries past pair_counts[m] are never read. `pair_counts`: some block has all 11 slots live.
All inputs are finite; a program needn't handle non-finite values.
Results may differ from a plain program's by a relative error of at most 0.00099.
Values may be sent and summed in bfloat16 or wider, within the bound.
No kernel may reach another device: no remote copies, remote signals or barrier semaphores. Data moves between devices by JAX's collectives and lax.ppermute only.
A program may use at most 192 MiB of HBM per device.

v0:
```python
import jax
import jax.numpy as jnp
from jax import lax
from jax.sharding import PartitionSpec as P


def slot_term(integral_block, picked):
    return jnp.einsum("pab,bi->pai", integral_block, picked, preferred_element_type=jnp.float32)


def zero_term(integral_block, picked):
    return jnp.zeros(
        (integral_block.shape[0], integral_block.shape[1], picked.shape[1]), jnp.float32
    )


def per_device(integrals, orbitals, pair_lists, pair_counts):
    local_ints = integrals[:, 0]
    width = orbitals.shape[0]
    columns = orbitals.shape[1]
    slot_total = pair_lists.shape[1]
    live = pair_counts[0]
    start_sum = jnp.zeros((local_ints.shape[0], width, columns), jnp.float32)
    carry = start_sum
    piece = lax.all_gather(orbitals, "blk", axis=0, tiled=True)
    piece_rows = piece.shape[0]
    for slot_index in range(slot_total):
        offset = pair_lists[0, slot_index] * width
        inside = (offset >= 0) & (offset < piece_rows) & (slot_index < live)
        picked = lax.dynamic_slice_in_dim(piece, jnp.clip(offset, 0, piece_rows - width), width, 0)
        carry = carry + lax.cond(inside, slot_term, zero_term, local_ints[:, slot_index], picked)
    halves = carry.astype(jnp.bfloat16)
    occ_total = columns * lax.axis_size("occ")
    partial_value = (
        jnp.einsum("pai,pbi->ab", halves, halves, preferred_element_type=jnp.float32) / occ_total
    )
    summed = lax.psum(partial_value, ("aux", "occ"))
    kept_rows = summed.shape[0] // lax.axis_size("aux")
    result = lax.dynamic_slice_in_dim(summed, lax.axis_index("aux") * kept_rows, kept_rows, 0)
    return result[None]


def solution(mesh):
    placed = (P("aux", "blk", None, None, None), P("blk", "occ"), P("blk", None), P("blk"))
    return jax.shard_map(
        per_device, mesh=mesh, in_specs=placed, out_specs=P("blk", "aux", None), check_vma=False
    )
```

profile of v0, /device:TPU:0, one launch (start us, length us, event | category | flops | bytes accessed | tf_op | source)
XLA Modules:
  0.0 163.6 jit_solution(8420829458339828189)
XLA Ops:
  6.5 1.8 %copy.5 = bf16[512,256]{0,1:T(8,128)(2,1)} copy(bf16[512,256]{1,0:T(8,128)(2,1)} %param.27) | data formatting | bytes 524288 | tf_op args[1]
  8.3 0.0 all-gather.2.cloned.1.call-update
  8.4 0.0 all-reduce.2.cloned.1.call-start
  8.4 1.7 %fusion.100 = (s32[1,1]{1,0:T(1,128)}, s32[1,1]{1,0:T(1,128)}, s32[1,1]{1,0:T(1,128)}, s32[1,1]{1,0:T(1,128)}, s32[1,1]{1,0:T(1,128)}, /*index=5*/s32[1,1]{1,0:T...) fusion(s32[1,11]{1,0:T(1,128)} %param.28), kind=kLoop, calls=%fused_computation.82 | loop fusion | bytes 88 | tf_op jit(solution)/shard_map/slice | solution.py:28
  17.7 20.0 %copy.12 = bf16[4,1,11,512,512]{4,3,0,2,1:T(8,128)(2,1)} copy(bf16[4,1,11,512,512]{4,3,2,1,0:T(8,128)(2,1)} %param.26) | data formatting | bytes 46137344 | tf_op args[0]
  37.6 2.0 %all-gather.2.cloned.1.call-done = bf16[2048,256]{0,1:T(8,128)(2,1)} async-done(((bf16[512,256]{0,1:T(8,128)(2,1)}), bf16[2048,256]{0,1:T(8,128)(2,1)}) %all-gather.2.cloned.1.call-update) | async-done | bytes 1048592 | tf_op jit(solution)/shard_map/all_gather | solution.py:25
  39.6 2.5 %conditional.11 = (f32[4,512,256]{1,2,0:T(8,128)S(1)}) conditional(s32[]{:T(128)} %convert_element_type.36, () %tuple.93, (s32[]{:T(128)}, bf16[2048,256]{0,1:T(8,128)(2,1)}, bf16[4,11,512,512]{3,2,0,1:T(8,128)(2,1)}) %tuple.151), branch_computations={%region_0.1_spmd, %region_1.2_spmd} | conditional | flops 536870912 | bytes 4456484 | solution.py:31
  39.6 2.5 %fusion.3 = f32[4,512,256]{1,2,0:T(8,128)S(1)} fusion(bf16[4,11,512,512]{3,2,0,1:T(8,128)(2,1)} %get-tuple-element.304, bf16[2048,256]{0,1:T(8,128)(2,1)} %get-tuple-element.302, s32[]{:T(128)S(6)} %min.45), kind=kOutput, calls=%fused_computation.3 | convolution fusion | flops 536870912 | bytes 4456452 | tf_op jit(solution)/shard_map/cond/branch_1_fun/pab,bi->pai/dot_general | solution.py:8
  42.1 3.9 %conditional.12 = (f32[4,512,256]{1,2,0:T(8,128)}) conditional(s32[]{:T(128)} %convert_element_type.37, () %tuple.95, (s32[]{:T(128)}, bf16[2048,256]{0,1:T(8,128)(2,1)}, bf16[4,11,512,512]{3,2,0,1:T(8,128)(2,1)}) %tuple.152), branch_computations={%region_2.3_spmd, %region_3.4_spmd} | conditional | flops 536870912 | bytes 4456484 | solution.py:31
  42.1 3.9 %fusion.12 = f32[4,512,256]{1,2,0:T(8,128)} fusion(bf16[4,11,512,512]{3,2,0,1:T(8,128)(2,1)} %get-tuple-element.307, bf16[2048,256]{0,1:T(8,128)(2,1)} %get-tuple-element.305, s32[]{:T(128)S(6)} %min.46), kind=kOutput, calls=%fused_computation.10 | convolution fusion | flops 536870912 | bytes 4456452 | tf_op jit(solution)/shard_map/cond/branch_1_fun/pab,bi->pai/dot_general | solution.py:8
  46.0 3.8 %conditional.13 = (f32[4,512,256]{1,2,0:T(8,128)}) conditional(s32[]{:T(128)} %convert_element_type.38, () %tuple.97, (s32[]{:T(128)}, bf16[2048,256]{0,1:T(8,128)(2,1)}, bf16[4,11,512,512]{3,2,0,1:T(8,128)(2,1)}) %tuple.153), branch_computations={%region_4.5_spmd, %region_5.6_spmd} | conditional | flops 536870912 | bytes 4456484 | solution.py:31
  46.0 3.8 %fusion.21 = f32[4,512,256]{1,2,0:T(8,128)} fusion(bf16[4,11,512,512]{3,2,0,1:T(8,128)(2,1)} %get-tuple-element.310, bf16[2048,256]{0,1:T(8,128)(2,1)} %get-tuple-element.308, s32[]{:T(128)S(6)} %min.47), kind=kOutput, calls=%fused_computation.17 | convolution fusion | flops 536870912 | bytes 4456452 | tf_op jit(solution)/shard_map/cond/branch_1_fun/pab,bi->pai/dot_general | solution.py:8
  49.9 3.8 %conditional.14 = (f32[4,512,256]{1,2,0:T(8,128)}) conditional(s32[]{:T(128)} %convert_element_type.39, () %tuple.99, (s32[]{:T(128)}, bf16[2048,256]{0,1:T(8,128)(2,1)}, bf16[4,11,512,512]{3,2,0,1:T(8,128)(2,1)}) %tuple.154), branch_computations={%region_6.7_spmd, %region_7.8_spmd} | conditional | flops 536870912 | bytes 4456484 | solution.py:31
  49.9 3.8 %fusion.30 = f32[4,512,256]{1,2,0:T(8,128)} fusion(bf16[4,11,512,512]{3,2,0,1:T(8,128)(2,1)} %get-tuple-element.313, bf16[2048,256]{0,1:T(8,128)(2,1)} %get-tuple-element.311, s32[]{:T(128)S(6)} %min.48), kind=kOutput, calls=%fused_computation.24 | convolution fusion | flops 536870912 | bytes 4456452 | tf_op jit(solution)/shard_map/cond/branch_1_fun/pab,bi->pai/dot_general | solution.py:8
  53.7 3.8 %conditional.15 = (f32[4,512,256]{1,2,0:T(8,128)}) conditional(s32[]{:T(128)} %convert_element_type.40, () %tuple.101, (s32[]{:T(128)}, bf16[2048,256]{0,1:T(8,128)(2,1)}, bf16[4,11,512,512]{3,2,0,1:T(8,128)(2,1)}) %tuple.155), branch_computations={%region_8.9_spmd, %region_9.10_spmd} | conditional | flops 536870912 | bytes 4456484 | solution.py:31
  53.7 3.8 %fusion.39 = f32[4,512,256]{1,2,0:T(8,128)} fusion(bf16[4,11,512,512]{3,2,0,1:T(8,128)(2,1)} %get-tuple-element.316, bf16[2048,256]{0,1:T(8,128)(2,1)} %get-tuple-element.314, s32[]{:T(128)S(6)} %min.49), kind=kOutput, calls=%fused_computation.31 | convolution fusion | flops 536870912 | bytes 4456452 | tf_op jit(solution)/shard_map/cond/branch_1_fun/pab,bi->pai/dot_general | solution.py:8
  57.4 3.8 %conditional.16 = (f32[4,512,256]{1,2,0:T(8,128)}) conditional(s32[]{:T(128)} %convert_element_type.41, () %tuple.103, (s32[]{:T(128)}, bf16[2048,256]{0,1:T(8,128)(2,1)}, bf16[4,11,512,512]{3,2,0,1:T(8,128)(2,1)}) %tuple.156), branch_computations={%region_10.11_spmd, %region_11.12_spmd} | conditional | flops 536870912 | bytes 4456484 | solution.py:31
  57.4 3.8 %fusion.48 = f32[4,512,256]{1,2,0:T(8,128)} fusion(bf16[4,11,512,512]{3,2,0,1:T(8,128)(2,1)} %get-tuple-element.319, bf16[2048,256]{0,1:T(8,128)(2,1)} %get-tuple-element.317, s32[]{:T(128)S(6)} %min.50), kind=kOutput, calls=%fused_computation.38 | convolution fusion | flops 536870912 | bytes 4456452 | tf_op jit(solution)/shard_map/cond/branch_1_fun/pab,bi->pai/dot_general | solution.py:8
  61.2 3.7 %conditional.17 = (f32[4,512,256]{1,2,0:T(8,128)}) conditional(s32[]{:T(128)} %convert_element_type.42, () %tuple.105, (s32[]{:T(128)}, bf16[2048,256]{0,1:T(8,128)(2,1)}, bf16[4,11,512,512]{3,2,0,1:T(8,128)(2,1)}) %tuple.157), branch_computations={%region_12.13_spmd, %region_13.14_spmd} | conditional | flops 536870912 | bytes 4456484 | solution.py:31
  61.2 3.7 %fusion.57 = f32[4,512,256]{1,2,0:T(8,128)} fusion(bf16[4,11,512,512]{3,2,0,1:T(8,128)(2,1)} %get-tuple-element.322, bf16[2048,256]{0,1:T(8,128)(2,1)} %get-tuple-element.320, s32[]{:T(128)S(6)} %min.51), kind=kOutput, calls=%fused_computation.45 | convolution fusion | flops 536870912 | bytes 4456452 | tf_op jit(solution)/shard_map/cond/branch_1_fun/pab,bi->pai/dot_general | solution.py:8
  65.0 3.8 %conditional.18 = (f32[4,512,256]{1,2,0:T(8,128)}) conditional(s32[]{:T(128)} %convert_element_type.43, () %tuple.107, (s32[]{:T(128)}, bf16[2048,256]{0,1:T(8,128)(2,1)}, bf16[4,11,512,512]{3,2,0,1:T(8,128)(2,1)}) %tuple.158), branch_computations={%region_14.15_spmd, %region_15.16_spmd} | conditional | flops 536870912 | bytes 4456484 | solution.py:31
  65.0 3.8 %fusion.66 = f32[4,512,256]{1,2,0:T(8,128)} fusion(bf16[4,11,512,512]{3,2,0,1:T(8,128)(2,1)} %get-tuple-element.325, bf16[2048,256]{0,1:T(8,128)(2,1)} %get-tuple-element.323, s32[]{:T(128)S(6)} %min.52), kind=kOutput, calls=%fused_computation.52 | convolution fusion | flops 536870912 | bytes 4456452 | tf_op jit(solution)/shard_map/cond/branch_1_fun/pab,bi->pai/dot_general | solution.py:8
  68.8 3.8 %conditional.19 = (f32[4,512,256]{1,2,0:T(8,128)}) conditional(s32[]{:T(128)} %convert_element_type.44, () %tuple.109, (s32[]{:T(128)}, bf16[2048,256]{0,1:T(8,128)(2,1)}, bf16[4,11,512,512]{3,2,0,1:T(8,128)(2,1)}) %tuple.159), branch_computations={%region_16.17_spmd, %region_17.18_spmd} | conditional | flops 536870912 | bytes 4456484 | solution.py:31
  68.8 3.8 %fusion.75 = f32[4,512,256]{1,2,0:T(8,128)} fusion(bf16[4,11,512,512]{3,2,0,1:T(8,128)(2,1)} %get-tuple-element.328, bf16[2048,256]{0,1:T(8,128)(2,1)} %get-tuple-element.326, s32[]{:T(128)S(6)} %min.53), kind=kOutput, calls=%fused_computation.59 | convolution fusion | flops 536870912 | bytes 4456452 | tf_op jit(solution)/shard_map/cond/branch_1_fun/pab,bi->pai/dot_general | solution.py:8
  72.6 3.8 %conditional.20 = (f32[4,512,256]{1,2,0:T(8,128)}) conditional(s32[]{:T(128)} %convert_element_type.45, () %tuple.111, (s32[]{:T(128)}, bf16[2048,256]{0,1:T(8,128)(2,1)}, bf16[4,11,512,512]{3,2,0,1:T(8,128)(2,1)}) %tuple.160), branch_computations={%region_18.19_spmd, %region_19.20_spmd} | conditional | flops 536870912 | bytes 4456484 | solution.py:31
  72.6 3.8 %fusion.84 = f32[4,512,256]{1,2,0:T(8,128)} fusion(bf16[4,11,512,512]{3,2,0,1:T(8,128)(2,1)} %get-tuple-element.331, bf16[2048,256]{0,1:T(8,128)(2,1)} %get-tuple-element.329, s32[]{:T(128)S(6)} %min.54), kind=kOutput, calls=%fused_computation.66 | convolution fusion | flops 536870912 | bytes 4456452 | tf_op jit(solution)/shard_map/cond/branch_1_fun/pab,bi->pai/dot_general | solution.py:8
  76.4 1.6 conditional.21
  76.4 1.6 broadcast.33
  78.0 18.2 %fusion.99 = f32[512,512]{1,0:T(8,128)} fusion(f32[4,512,256]{1,2,0:T(8,128)} %get-tuple-element.356, f32[4,512,256]{1,2,0:T(8,128)} %get-tuple-element.355, f32[4,512,256]{1,2,0:T(8,128)} %get-tuple-element.354, f32[4,512,256]{1,2,0:T(8,128)} %get-tuple-element.353, f32[4,512,256]{1,2,0:T(8,128)} %get-tuple-element.352, ...), kind=kOutput, calls=%fused_computation.80 | convolution fusion | flops 542900224 | bytes 24117248 | tf_op jit(solution)/shard_map/pai,pbi->ab/dot_general | solution.py:35
  96.2 0.0 all-reduce.2.cloned.1.call-update
  96.3 58.8 %all-reduce.2.cloned.1.call-done = f32[512,512]{1,0:T(8,128)} async-done(((f32[512,512]{1,0:T(8,128)}), f32[512,512]{1,0:T(8,128)}) %all-reduce.2.cloned.1.call-update) | async-done | bytes 1048592 | tf_op jit(solution)/shard_map/psum | solution.py:37
  155.0 1.7 %dynamic-slice_bitcast_fusion = f32[1,128,512]{2,1,0:T(8,128)} fusion(f32[512,512]{1,0:T(8,128)} %all-reduce.2.cloned.1.call-done, s32[]{:T(128)S(6)} %select_n.2), kind=kLoop, calls=%fused_computation.81 | loop fusion | bytes 524292 | tf_op jit(solution)/shard_map/broadcast_in_dim | solution.py:40
  (1 shorter events, 0.0 us)
Async XLA Ops:
  6.5 33.1 %all-gather.2.cloned.1.call-start = ((), (), s32[]{:S(2)}) async-start(), calls=%async_computation | async-start | bytes 1310720 | tf_op jit(solution)/shard_map/all_gather | solution.py:25
  8.4 146.7 %all-reduce.2.cloned.1.call-start = ((), (), s32[]{:S(2)}) async-start(), calls=%async_computation.1 | async-start | bytes 2097152 | tf_op jit(solution)/shard_map/psum | solution.py:37
Sparse Core Ops, SparseCore 0:
  8.9 30.6 all-gather.1
  96.4 58.6 all-reduce.1
where the time goes:
time: 164 us
  waiting for transfers between devices  60.8 us (37%)
  matrix products  54.9 us (33%)
  local copies, waits for them, and re-layouts  26.8 us (16%)
  between operations  20.9 us (13%)
    psum x1, waiting for transfers between devices, per_device(): summed = lax.psum(partial_value, ('aux', 'occ'))  58.8 us
    dot_general x10, matrix products, slot_term(): jnp.einsum('pab,bi->pai', integral_block, picked, preferred_element_type=...  36.7 us
    unnamed x2, local copies, waits for them, and re-layouts  21.8 us
    dot_general x1, matrix products, per_device(): jnp.einsum('pai,pbi->ab', halves, halves, preferred_element_type=jnp.floa...  18.2 us
  transfers between devices with their start and end apart: 2, of which 2 were waited for; matrix products, arithmetic and copies ran while one was open for 13% of the time, Pallas kernels for 0%

commit v1 on v0

--- a/solution.py
+++ b/solution.py
@@ -2,6 +2,12 @@
 import jax.numpy as jnp
 from jax import lax
 from jax.sharding import PartitionSpec as P
+
+
+def write_the_skins(field, shard_axis, across):
+    for pp in (shard_axis, across):
+        field = lax.psum(field, axis_name=pp)
+    return field
 
 
 def slot_term(integral_block, picked):
@@ -34,7 +40,7 @@
     partial_value = (
         jnp.einsum("pai,pbi->ab", halves, halves, preferred_element_type=jnp.float32) / occ_total
     )
-    summed = lax.psum(partial_value, ("aux", "occ"))
+    summed = write_the_skins(partial_value, "occ", "aux")
     kept_rows = summed.shape[0] // lax.axis_size("aux")
     result = lax.dynamic_slice_in_dim(summed, lax.axis_index("aux") * kept_rows, kept_rows, 0)
     return result[None]

time: 164 us -> 184 us (1.12)
  waiting for transfers between devices: 60.8 us -> 80.3 us
    psum x1 -> x2, waiting for transfers between devices: 58.8 us -> 78.2 us  [write_the_skins(): field = lax.psum(field, axis_name=pp)]
  transfers between devices with their start and end apart: 2 -> 3, of which waited for: 2 -> 3; matrix products, arithmetic and copies ran while one was open for 13% -> 12% of each run, Pallas kernels for 0% -> 0%
where the time goes in v1:
time: 184 us; the launch traced here: 183 us
  waiting for transfers between devices  80.3 us (44%)
  matrix products  54.9 us (30%)
  local copies, waits for them, and re-layouts  26.8 us (15%)
  between operations  20.6 us (11%)
    psum x2, waiting for transfers between devices, write_the_skins(): field = lax.psum(field, axis_name=pp)  78.2 us
    dot_general x10, matrix products, slot_term(): jnp.einsum('pab,bi->pai', integral_block, picked, preferred_element_type=...  36.7 us
    unnamed x2, local copies, waits for them, and re-layouts  21.8 us
    dot_general x1, matrix products, per_device(): jnp.einsum('pai,pbi->ab', halves, halves, preferred_element_type=jnp.floa...  18.2 us
  transfers between devices with their start and end apart: 3, of which 3 were waited for; matrix products, arithmetic and copies ran while one was open for 12% of the time, Pallas kernels for 0%

profile of v1, /device:TPU:0, one launch (start us, length us, event | category | flops | bytes accessed | tf_op | source)
XLA Modules:
  0.0 182.7 jit_solution(13204741147665166352)
XLA Ops:
  6.5 1.8 copy.5
  8.4 0.0 all-reduce.3.cloned.1.call-start
  8.4 1.7 fusion.100
  17.7 20.0 %copy.12 = bf16[4,1,11,512,512]{4,3,0,2,1:T(8,128)(2,1)} copy(bf16[4,1,11,512,512]{4,3,2,1,0:T(8,128)(2,1)} %param.26) | data formatting | bytes 46137344 | tf_op args[0]
  37.6 2.0 %all-gather.2.cloned.1.call-done = bf16[2048,256]{0,1:T(8,128)(2,1)} async-done(((bf16[512,256]{0,1:T(8,128)(2,1)}), bf16[2048,256]{0,1:T(8,128)(2,1)}) %all-gather.2.cloned.1.call-update) | async-done | bytes 1048592 | tf_op jit(solution)/shard_map/all_gather | solution.py:31
  39.6 2.5 %conditional.11 = (f32[4,512,256]{1,2,0:T(8,128)S(1)}) conditional(s32[]{:T(128)} %convert_element_type.36, () %tuple.93, (s32[]{:T(128)}, bf16[2048,256]{0,1:T(8,128)(2,1)}, bf16[4,11,512,512]{3,2,0,1:T(8,128)(2,1)}) %tuple.153), branch_computations={%region_0.1_spmd, %region_1.2_spmd} | conditional | flops 536870912 | bytes 4456484 | solution.py:37
  39.6 2.5 %fusion.3 = f32[4,512,256]{1,2,0:T(8,128)S(1)} fusion(bf16[4,11,512,512]{3,2,0,1:T(8,128)(2,1)} %get-tuple-element.304, bf16[2048,256]{0,1:T(8,128)(2,1)} %get-tuple-element.302, s32[]{:T(128)S(6)} %min.45), kind=kOutput, calls=%fused_computation.3 | convolution fusion | flops 536870912 | bytes 4456452 | tf_op jit(solution)/shard_map/cond/branch_1_fun/pab,bi->pai/dot_general | solution.py:14
  42.1 3.9 %conditional.12 = (f32[4,512,256]{1,2,0:T(8,128)}) conditional(s32[]{:T(128)} %convert_element_type.37, () %tuple.95, (s32[]{:T(128)}, bf16[2048,256]{0,1:T(8,128)(2,1)}, bf16[4,11,512,512]{3,2,0,1:T(8,128)(2,1)}) %tuple.154), branch_computations={%region_2.3_spmd, %region_3.4_spmd} | conditional | flops 536870912 | bytes 4456484 | solution.py:37
  42.1 3.9 %fusion.12 = f32[4,512,256]{1,2,0:T(8,128)} fusion(bf16[4,11,512,512]{3,2,0,1:T(8,128)(2,1)} %get-tuple-element.307, bf16[2048,256]{0,1:T(8,128)(2,1)} %get-tuple-element.305, s32[]{:T(128)S(6)} %min.46), kind=kOutput, calls=%fused_computation.10 | convolution fusion | flops 536870912 | bytes 4456452 | tf_op jit(solution)/shard_map/cond/branch_1_fun/pab,bi->pai/dot_general | solution.py:14
  46.0 3.8 %conditional.13 = (f32[4,512,256]{1,2,0:T(8,128)}) conditional(s32[]{:T(128)} %convert_element_type.38, () %tuple.97, (s32[]{:T(128)}, bf16[2048,256]{0,1:T(8,128)(2,1)}, bf16[4,11,512,512]{3,2,0,1:T(8,128)(2,1)}) %tuple.155), branch_computations={%region_4.5_spmd, %region_5.6_spmd} | conditional | flops 536870912 | bytes 4456484 | solution.py:37
  46.0 3.8 %fusion.21 = f32[4,512,256]{1,2,0:T(8,128)} fusion(bf16[4,11,512,512]{3,2,0,1:T(8,128)(2,1)} %get-tuple-element.310, bf16[2048,256]{0,1:T(8,128)(2,1)} %get-tuple-element.308, s32[]{:T(128)S(6)} %min.47), kind=kOutput, calls=%fused_computation.17 | convolution fusion | flops 536870912 | bytes 4456452 | tf_op jit(solution)/shard_map/cond/branch_1_fun/pab,bi->pai/dot_general | solution.py:14
  49.9 3.8 %conditional.14 = (f32[4,512,256]{1,2,0:T(8,128)}) conditional(s32[]{:T(128)} %convert_element_type.39, () %tuple.99, (s32[]{:T(128)}, bf16[2048,256]{0,1:T(8,128)(2,1)}, bf16[4,11,512,512]{3,2,0,1:T(8,128)(2,1)}) %tuple.156), branch_computations={%region_6.7_spmd, %region_7.8_spmd} | conditional | flops 536870912 | bytes 4456484 | solution.py:37
  49.9 3.8 %fusion.30 = f32[4,512,256]{1,2,0:T(8,128)} fusion(bf16[4,11,512,512]{3,2,0,1:T(8,128)(2,1)} %get-tuple-element.313, bf16[2048,256]{0,1:T(8,128)(2,1)} %get-tuple-element.311, s32[]{:T(128)S(6)} %min.48), kind=kOutput, calls=%fused_computation.24 | convolution fusion | flops 536870912 | bytes 4456452 | tf_op jit(solution)/shard_map/cond/branch_1_fun/pab,bi->pai/dot_general | solution.py:14
  53.7 3.8 %conditional.15 = (f32[4,512,256]{1,2,0:T(8,128)}) conditional(s32[]{:T(128)} %convert_element_type.40, () %tuple.101, (s32[]{:T(128)}, bf16[2048,256]{0,1:T(8,128)(2,1)}, bf16[4,11,512,512]{3,2,0,1:T(8,128)(2,1)}) %tuple.157), branch_computations={%region_8.9_spmd, %region_9.10_spmd} | conditional | flops 536870912 | bytes 4456484 | solution.py:37
  53.7 3.8 %fusion.39 = f32[4,512,256]{1,2,0:T(8,128)} fusion(bf16[4,11,512,512]{3,2,0,1:T(8,128)(2,1)} %get-tuple-element.316, bf16[2048,256]{0,1:T(8,128)(2,1)} %get-tuple-element.314, s32[]{:T(128)S(6)} %min.49), kind=kOutput, calls=%fused_computation.31 | convolution fusion | flops 536870912 | bytes 4456452 | tf_op jit(solution)/shard_map/cond/branch_1_fun/pab,bi->pai/dot_general | solution.py:14
  57.4 3.8 %conditional.16 = (f32[4,512,256]{1,2,0:T(8,128)}) conditional(s32[]{:T(128)} %convert_element_type.41, () %tuple.103, (s32[]{:T(128)}, bf16[2048,256]{0,1:T(8,128)(2,1)}, bf16[4,11,512,512]{3,2,0,1:T(8,128)(2,1)}) %tuple.158), branch_computations={%region_10.11_spmd, %region_11.12_spmd} | conditional | flops 536870912 | bytes 4456484 | solution.py:37
  57.4 3.8 %fusion.48 = f32[4,512,256]{1,2,0:T(8,128)} fusion(bf16[4,11,512,512]{3,2,0,1:T(8,128)(2,1)} %get-tuple-element.319, bf16[2048,256]{0,1:T(8,128)(2,1)} %get-tuple-element.317, s32[]{:T(128)S(6)} %min.50), kind=kOutput, calls=%fused_computation.38 | convolution fusion | flops 536870912 | bytes 4456452 | tf_op jit(solution)/shard_map/cond/branch_1_fun/pab,bi->pai/dot_general | solution.py:14
  61.2 3.7 %conditional.17 = (f32[4,512,256]{1,2,0:T(8,128)}) conditional(s32[]{:T(128)} %convert_element_type.42, () %tuple.105, (s32[]{:T(128)}, bf16[2048,256]{0,1:T(8,128)(2,1)}, bf16[4,11,512,512]{3,2,0,1:T(8,128)(2,1)}) %tuple.159), branch_computations={%region_12.13_spmd, %region_13.14_spmd} | conditional | flops 536870912 | bytes 4456484 | solution.py:37
  61.2 3.7 %fusion.57 = f32[4,512,256]{1,2,0:T(8,128)} fusion(bf16[4,11,512,512]{3,2,0,1:T(8,128)(2,1)} %get-tuple-element.322, bf16[2048,256]{0,1:T(8,128)(2,1)} %get-tuple-element.320, s32[]{:T(128)S(6)} %min.51), kind=kOutput, calls=%fused_computation.45 | convolution fusion | flops 536870912 | bytes 4456452 | tf_op jit(solution)/shard_map/cond/branch_1_fun/pab,bi->pai/dot_general | solution.py:14
  65.0 3.8 %conditional.18 = (f32[4,512,256]{1,2,0:T(8,128)}) conditional(s32[]{:T(128)} %convert_element_type.43, () %tuple.107, (s32[]{:T(128)}, bf16[2048,256]{0,1:T(8,128)(2,1)}, bf16[4,11,512,512]{3,2,0,1:T(8,128)(2,1)}) %tuple.160), branch_computations={%region_14.15_spmd, %region_15.16_spmd} | conditional | flops 536870912 | bytes 4456484 | solution.py:37
  65.0 3.8 %fusion.66 = f32[4,512,256]{1,2,0:T(8,128)} fusion(bf16[4,11,512,512]{3,2,0,1:T(8,128)(2,1)} %get-tuple-element.325, bf16[2048,256]{0,1:T(8,128)(2,1)} %get-tuple-element.323, s32[]{:T(128)S(6)} %min.52), kind=kOutput, calls=%fused_computation.52 | convolution fusion | flops 536870912 | bytes 4456452 | tf_op jit(solution)/shard_map/cond/branch_1_fun/pab,bi->pai/dot_general | solution.py:14
  68.8 3.8 %conditional.19 = (f32[4,512,256]{1,2,0:T(8,128)}) conditional(s32[]{:T(128)} %convert_element_type.44, () %tuple.109, (s32[]{:T(128)}, bf16[2048,256]{0,1:T(8,128)(2,1)}, bf16[4,11,512,512]{3,2,0,1:T(8,128)(2,1)}) %tuple.161), branch_computations={%region_16.17_spmd, %region_17.18_spmd} | conditional | flops 536870912 | bytes 4456484 | solution.py:37
  68.8 3.8 %fusion.75 = f32[4,512,256]{1,2,0:T(8,128)} fusion(bf16[4,11,512,512]{3,2,0,1:T(8,128)(2,1)} %get-tuple-element.328, bf16[2048,256]{0,1:T(8,128)(2,1)} %get-tuple-element.326, s32[]{:T(128)S(6)} %min.53), kind=kOutput, calls=%fused_computation.59 | convolution fusion | flops 536870912 | bytes 4456452 | tf_op jit(solution)/shard_map/cond/branch_1_fun/pab,bi->pai/dot_general | solution.py:14
  72.6 3.8 %conditional.20 = (f32[4,512,256]{1,2,0:T(8,128)}) conditional(s32[]{:T(128)} %convert_element_type.45, () %tuple.111, (s32[]{:T(128)}, bf16[2048,256]{0,1:T(8,128)(2,1)}, bf16[4,11,512,512]{3,2,0,1:T(8,128)(2,1)}) %tuple.162), branch_computations={%region_18.19_spmd, %region_19.20_spmd} | conditional | flops 536870912 | bytes 4456484 | solution.py:37
  72.6 3.8 %fusion.84 = f32[4,512,256]{1,2,0:T(8,128)} fusion(bf16[4,11,512,512]{3,2,0,1:T(8,128)(2,1)} %get-tuple-element.331, bf16[2048,256]{0,1:T(8,128)(2,1)} %get-tuple-element.329, s32[]{:T(128)S(6)} %min.54), kind=kOutput, calls=%fused_computation.66 | convolution fusion | flops 536870912 | bytes 4456452 | tf_op jit(solution)/shard_map/cond/branch_1_fun/pab,bi->pai/dot_general | solution.py:14
  76.4 1.6 conditional.21
  76.4 1.6 broadcast.33
  78.0 18.2 %fusion.99 = f32[512,512]{1,0:T(8,128)} fusion(f32[4,512,256]{1,2,0:T(8,128)} %get-tuple-element.356, f32[4,512,256]{1,2,0:T(8,128)} %get-tuple-element.355, f32[4,512,256]{1,2,0:T(8,128)} %get-tuple-element.354, f32[4,512,256]{1,2,0:T(8,128)} %get-tuple-element.353, f32[4,512,256]{1,2,0:T(8,128)} %get-tuple-element.352, ...), kind=kOutput, calls=%fused_computation.80 | convolution fusion | flops 542900224 | bytes 24117248 | tf_op jit(solution)/shard_map/pai,pbi->ab/dot_general | solution.py:41
  96.3 0.0 all-reduce.5.cloned.1.call-start
  96.3 21.5 %all-reduce.3.cloned.1.call-done = f32[512,512]{1,0:T(8,128)} async-done(((f32[512,512]{1,0:T(8,128)}), f32[512,512]{1,0:T(8,128)}) %all-reduce.3.cloned.1.call-update) | async-done | bytes 1048592 | tf_op jit(solution)/shard_map/psum | solution.py:9
  117.8 56.7 %all-reduce.5.cloned.1.call-done = f32[512,512]{1,0:T(8,128)} async-done(((f32[512,512]{1,0:T(8,128)}), f32[512,512]{1,0:T(8,128)}) %all-reduce.5.cloned.1.call-update) | async-done | bytes 1048592 | tf_op jit(solution)/shard_map/psum | solution.py:9
  174.5 1.7 dynamic-slice_bitcast_fusion
  (4 shorter events, 0.1 us)
Async XLA Ops:
  6.5 33.1 %all-gather.2.cloned.1.call-start = ((), (), s32[]{:S(2)}) async-start(), calls=%async_computation | async-start | bytes 1310720 | tf_op jit(solution)/shard_map/all_gather | solution.py:31
  8.4 109.4 %all-reduce.3.cloned.1.call-start = ((), (), s32[]{:S(2)}) async-start(), calls=%async_computation.1 | async-start | bytes 2097152 | tf_op jit(solution)/shard_map/psum | solution.py:9
  96.3 78.3 %all-reduce.5.cloned.1.call-start = ((), (), s32[]{:S(2)}) async-start(), calls=%async_computation.2 | async-start | bytes 2097152 | tf_op jit(solution)/shard_map/psum | solution.py:9
Sparse Core Ops, SparseCore 0:
  8.9 30.6 all-gather.1
  96.4 21.3 all-reduce.2
  120.9 53.6 all-reduce.4
